TPU v7x, 32 devices: a whole 2x2x4 slice. The times are simulated.
32 devices in a mesh: ctx: 8 (over z, y), chan: 4 (over x, core).
Axes of the slice: x: 2, y: 2, z: 4, core: 2. Of those that a mesh axis runs over, the one named last changes fastest.
Arguments:
- tokens: bfloat16 [2048, 4096], P('ctx', 'chan'), may hold values from -6 to 6
- gain: float32 [4096], replicated, may hold values from 0.1 to 1.9
- in_weight: bfloat16 [3, 4096, 2048], P(None, None, 'chan'), may hold values from -0.09375 to 0.09375
- short_weight: float32 [3, 3, 2048], P(None, None, 'chan'), may hold values from -3.5 to 3.5
- residues: float32 [16, 2048], P(None, 'chan'), may hold values from -1.5 to 1.5
- rates: float32 [16, 2048], P(None, 'chan'), may hold values from 0.1 to 51
- out_weight: bfloat16 [2048, 4096], P('chan'), may hold values from -0.1875 to 0.1875
Outputs:
- mixed: bfloat16 [2048, 4096], P('ctx', 'chan')
All inputs are finite; a program needn't handle non-finite values.
Results may differ from a plain program's by a relative error of at most 0.018.
Values may be sent and summed in bfloat16 or wider, within the bound.
A program may use at most 128 MiB of HBM per device.

v0:
```python
import math

import jax
import jax.numpy as jnp
from jax import lax
from jax.sharding import PartitionSpec as P

highest = lax.Precision.HIGHEST
two_pi = 2.0 * math.pi


def shortened(shard):

    def short(part):
        return part.astype(jnp.bfloat16) if part.dtype == jnp.float32 else part

    return jax.tree.map(short, shard)


def from_behind(shard, axis, by):
    peers = lax.axis_size(axis)
    pairs = [(i, i + by) for i in range(peers) if 0 <= i + by < peers]
    return lax.ppermute(shard, axis, pairs)


def turn_angle(first, second, modulus):
    return (first * second % modulus).astype(jnp.float32) * (two_pi / modulus)


def local_forward(spectra, freq_slots, padded_length):
    row_count = spectra.shape[3]
    steps_idx = jnp.arange(row_count, dtype=jnp.int32)
    twiddle = turn_angle(freq_slots[:, None], steps_idx[None, :], padded_length)[:, :, None]
    cosine_term = jnp.cos(twiddle)
    sine_term = jnp.sin(twiddle)
    real_part = spectra[:, 0]
    imag_part = spectra[:, 1]
    turned_real = real_part * cosine_term + imag_part * sine_term
    turned_imag = imag_part * cosine_term - real_part * sine_term
    stacked = jnp.concatenate([turned_real, turned_imag], axis=2)
    dft_angle = turn_angle(steps_idx[:, None], steps_idx[None, :], row_count)
    cos_table = jnp.cos(dft_angle)
    sin_table = jnp.sin(dft_angle)
    block_table = jnp.concatenate(
        [
            jnp.concatenate([cos_table, sin_table], axis=1),
            jnp.concatenate([-sin_table, cos_table], axis=1),
        ],
        axis=0,
    )
    both_parts = jnp.einsum("pj,fsjc->fspc", block_table, stacked, precision=highest)
    return (both_parts[:, :, :row_count], both_parts[:, :, row_count:])


def local_inverse(spec_real, spec_imag, freq_slots, padded_length):
    row_count = spec_real.shape[1]
    steps_idx = jnp.arange(row_count, dtype=jnp.int32)
    dft_angle = turn_angle(steps_idx[:, None], steps_idx[None, :], row_count)
    cos_table = jnp.cos(dft_angle)
    sin_table = jnp.sin(dft_angle)
    block_table = jnp.concatenate(
        [
            jnp.concatenate([cos_table, -sin_table], axis=1),
            jnp.concatenate([sin_table, cos_table], axis=1),
        ],
        axis=0,
    )
    stacked = jnp.concatenate([spec_real, spec_imag], axis=1)
    both_parts = jnp.einsum("jp,spc->sjc", block_table, stacked, precision=highest) / row_count
    back_real = both_parts[:, :row_count]
    back_imag = both_parts[:, row_count:]
    twiddle = turn_angle(freq_slots[:, None], steps_idx[None, :], padded_length)[:, :, None]
    cosine_term = jnp.cos(twiddle)
    sine_term = jnp.sin(twiddle)
    return (
        back_real * cosine_term - back_imag * sine_term,
        back_imag * cosine_term + back_real * sine_term,
    )


def across_blocks(received, sample_ids, freq_count):
    freq_ids = jnp.arange(freq_count, dtype=jnp.int32)
    rotation = turn_angle(freq_ids[:, None], sample_ids[None, :], freq_count)
    real_part = jnp.einsum("qm,fmjc->fqjc", jnp.cos(rotation), received, precision=highest)
    imag_part = -jnp.einsum("qm,fmjc->fqjc", jnp.sin(rotation), received, precision=highest)
    return jnp.stack([real_part, imag_part], axis=1)


def rows_from_spectra(received, sample_ids, freq_count):
    freq_ids = jnp.arange(freq_count, dtype=jnp.int32)
    rotation = turn_angle(sample_ids[:, None], freq_ids[None, :], freq_count)
    real_rows = jnp.einsum("mq,qjc->mjc", jnp.cos(rotation), received[0], precision=highest)
    real_rows = real_rows - jnp.einsum(
        "mq,qjc->mjc", jnp.sin(rotation), received[1], precision=highest
    )
    return real_rows / freq_count


def halved_forward(signal, device_index, group_size):
    received = lax.all_to_all(
        signal[:, None].astype(jnp.bfloat16), "ctx", split_axis=2, concat_axis=1, tiled=True
    ).astype(jnp.float32)
    spectra = across_blocks(received, jnp.arange(group_size, dtype=jnp.int32), 2 * group_size)
    gathered = lax.all_to_all(
        shortened(spectra), "ctx", split_axis=2, concat_axis=3, tiled=True
    ).astype(spectra.dtype)
    return (gathered, 2 * device_index + jnp.arange(2, dtype=jnp.int32))


def halved_inverse(spec_real, spec_imag, group_size):
    received = lax.all_to_all(
        shortened(jnp.stack([spec_real, spec_imag], axis=0)),
        "ctx",
        split_axis=2,
        concat_axis=1,
        tiled=True,
    )
    real_rows = rows_from_spectra(received, jnp.arange(group_size, dtype=jnp.int32), 2 * group_size)
    returned = lax.all_to_all(
        shortened(real_rows), "ctx", split_axis=0, concat_axis=1, tiled=True
    ).astype(real_rows.dtype)
    return returned[0]


def shards(tokens, gain, in_weight, short_weight, residues, rates, out_weight):
    features_all = lax.all_gather(tokens, "chan", axis=1, tiled=True)
    wide_rows = features_all.astype(jnp.float32)
    scale_rms = lax.rsqrt(jnp.mean(wide_rows * wide_rows, axis=-1, keepdims=True) + 1e-06)
    normed = (wide_rows * scale_rms * gain).astype(jnp.bfloat16)
    projected = jnp.einsum(
        "td,gdc->gtc", normed, in_weight, preferred_element_type=jnp.float32
    ).astype(jnp.bfloat16)
    row_count = projected.shape[1]
    rim_size = short_weight.shape[1] - 1
    rim_rows = from_behind(projected[:, row_count - rim_size :, :], "ctx", 1)
    extended = jnp.concatenate([rim_rows, projected], axis=1).astype(jnp.float32)
    filtered = jnp.zeros((3, row_count, projected.shape[2]), jnp.float32)
    for i in range(rim_size + 1):
        filtered = (
            filtered
            + short_weight[:, i][:, None, :] * extended[:, rim_size - i : rim_size - i + row_count]
        )
    drive_term = filtered[1] * filtered[2]
    group_size = lax.axis_size("ctx")
    device_index = lax.axis_index("ctx")
    length = row_count * group_size
    padded_length = 2 * length
    decay_rate = rates / length
    amplitude = residues * jnp.sqrt(-jnp.expm1(-2.0 * decay_rate))
    positions = (device_index * row_count + jnp.arange(row_count, dtype=jnp.int32)).astype(
        jnp.float32
    )
    kernel = jnp.sum(
        amplitude[:, None, :] * jnp.exp(-decay_rate[:, None, :] * positions[None, :, None]), axis=0
    )
    signal = jnp.stack([drive_term, kernel], axis=0)
    spectra, freq_slots = halved_forward(signal, device_index, group_size)
    spec_real, spec_imag = local_forward(spectra, freq_slots, padded_length)
    resp_real = spec_real[1]
    resp_imag = spec_imag[1]
    prod_real = spec_real[0] * resp_real - spec_imag[0] * resp_imag
    prod_imag = spec_real[0] * resp_imag + spec_imag[0] * resp_real
    back_real, back_imag = local_inverse(prod_real, prod_imag, freq_slots, padded_length)
    convolved = halved_inverse(back_real, back_imag, group_size)
    gated_rows = (filtered[0] * convolved).astype(jnp.bfloat16)
    partial_sums = jnp.dot(gated_rows, out_weight, preferred_element_type=jnp.float32)
    return lax.psum_scatter(
        partial_sums.astype(jnp.bfloat16), "chan", scatter_dimension=1, tiled=True
    )


def solution(mesh):
    return jax.shard_map(
        shards,
        mesh=mesh,
        in_specs=(
            P("ctx", "chan"),
            P(),
            P(None, None, "chan"),
            P(None, None, "chan"),
            P(None, "chan"),
            P(None, "chan"),
            P("chan", None),
        ),
        out_specs=P("ctx", "chan"),
        check_vma=False,
    )
```

profile of v0, /device:TPU:0, one launch (start us, length us, event | category | flops | bytes accessed | tf_op | source)
XLA Modules:
  0.0 229.2 jit_solution(4837787021221969557)
XLA Ops:
  6.5 0.7 all-gather.2.cloned.1.call-update
  7.3 0.9 fusion.110
  8.1 0.8 sqrt_multiply_fusion
  9.0 1.4 multiply_reduce_fusion
  10.4 23.8 %all-gather.2.cloned.1.call-done = bf16[256,4096]{1,0:T(8,128)(2,1)} async-done(((bf16[256,1024]{1,0:T(8,128)(2,1)}), bf16[256,4096]{1,0:T(8,128)(2,1)}) %all-gather.2.cloned.1.call-update) | async-done | bytes 2097168 | tf_op jit(solution)/shard_map/all_gather | solution.py:126
  34.2 2.2 fusion
  36.5 6.6 %fusion.28 = bf16[3,256,512]{2,1,0:T(8,128)(2,1)S(1)} fusion(bf16[3,4096,512]{2,1,0:T(8,128)(2,1)} %param.9, bf16[256,4096]{1,0:T(8,128)(2,1)S(1)} %copy-done.2, f32[4096]{0:T(1024)S(1)} %copy-done.3, f32[256]{0:T(256)S(1)} %add_rsqrt_fusion), kind=kOutput, calls=%fused_computation.40 | convolution fusion | flops 3225812992 | bytes 15483904 | tf_op jit(solution)/shard_map/td,gdc->gtc/dot_general | solution.py:130
  43.1 3.4 %collective-permute-start = (bf16[3,2,512]{2,1,0:T(2,128)(2,1)S(1)}, bf16[3,2,512]{2,1,0:T(2,128)(2,1)S(1)}, u32[]{:S(2)}, u32[]{:S(2)}) collective-permute-start(bf16[3,2,512]{2,1,0:T(2,128)(2,1)S(1)} %slice.90), channel_id=1, source_target_pairs={{0,4},{4,8},{8,12},{12,16},{16,20},{20,24},{24,28},{1,5},{5,9},{9,... | collective-permute-start | bytes 18440 | tf_op jit(solution)/shard_map/ppermute | solution.py:23
  46.5 1.3 collective-permute-done
  48.1 0.5 fusion.21
  48.7 0.5 copy.56
  49.2 19.9 %all_to_all.45 = bf16[2,1,256,512]{3,0,1,2:T(2,128)(2,1)S(1)} all-to-all(bf16[2,1,256,512]{3,0,1,2:T(2,128)(2,1)S(1)} %copy.56), channel_id=1, replica_groups=mesh['ctx'=8,'chan'=4] {'ctx'}, dimensions={2} | all-to-all | bytes 1048576 | tf_op jit(solution)/shard_map/all_to_all | solution.py:100
  69.2 1.1 fusion.26
  70.3 1.1 fusion.27
  71.6 2.5 %copy.60 = bf16[2,2,16,32,512]{4,3,0,1,2:T(8,128)(2,1)} copy(bf16[2,2,16,32,512]{4,2,3,0,1:T(8,128)(2,1)S(1)} %pad_maximum_fusion) | data formatting | bytes 4194304 | tf_op jit(solution)/shard_map/stack | solution.py:86
  74.1 3.6 %all-to-all-start.1 = ((bf16[2,2,16,32,512]{4,3,0,1,2:T(8,128)(2,1)}), bf16[2,2,16,32,512]{4,3,0,1,2:T(8,128)(2,1)S(1)}, u32[]{:S(2)}, u32[]{:S(2)}) async-start(bf16[2,2,16,32,512]{4,3,0,1,2:T(8,128)(2,1)} %copy.60), calls=%async_computation.1 | async-start | bytes 4194304 | tf_op jit(solution)/shard_map/all_to_all | solution.py:104
  78.0 1.0 fusion.60
  79.0 1.0 fusion.58
  80.2 45.4 %all-to-all-done.1 = bf16[2,2,16,32,512]{4,3,0,1,2:T(8,128)(2,1)S(1)} async-done(((bf16[2,2,16,32,512]{4,3,0,1,2:T(8,128)(2,1)}), bf16[2,2,16,32,512]{4,3,0,1,2:T(8,128)(2,1)S(1)}, u32[]{:S(2)}, u32[]{:S(2)}) %all-to-all-start.1) | async-done | bytes 2097184 | tf_op jit(solution)/shard_map/all_to_all | solution.py:104
  125.5 0.6 copy.61
  126.1 0.5 multiply_add_fusion
  126.6 7.9 %fusion.7 = f32[2,2,512,512]{3,2,1,0:T(8,128)S(1)} fusion(f32[2,2,256,512]{3,2,1,0:T(8,128)S(1)} %get-tuple-element.6, f32[2,2,256,512]{3,2,1,0:T(8,128)S(1)} %get-tuple-element.5, f32[256,256]{1,0:T(8,128)S(1)} %get-tuple-element.23, f32[256,256]{1,0:T(8,128)S(1)} %fusion.60, f32[256,256]{1,0:T(8,128)S(1)} %get-tuple-element.22), kind=kOutput, calls=%fused_computation.11 | convolution fusion | flops 6444285952 | bytes 9175040 | tf_op jit(solution)/shard_map/pj,fsjc->fspc/dot_general | solution.py:51
  134.6 0.5 subtract_bitcast_fusion
  135.1 7.1 %multiply_bitcast_fusion = f32[2,512,512]{1,2,0:T(8,128)S(1)} fusion(f32[2,256,512]{2,1,0:T(8,128)S(1)} %get-tuple-element.8, f32[2,256,512]{2,1,0:T(8,128)S(1)} %get-tuple-element.7, f32[256,256]{1,0:T(8,128)S(1)} %get-tuple-element.23, f32[256,256]{1,0:T(8,128)S(1)} %get-tuple-element.22, f32[256,256]{1,0:T(8,128)S(1)} %fusion.60), kind=kOutput, calls=%fused_computation.21 | convolution fusion | flops 3223060480 | bytes 4980736 | tf_op jit(solution)/shard_map/jp,spc->sjc/dot_general | solution.py:69
  142.6 1.1 copy.63
  143.7 29.3 %all_to_all.46 = bf16[2,2,256,512]{3,1,0,2:T(2,128)(2,1)S(1)} all-to-all(bf16[2,2,256,512]{3,1,0,2:T(2,128)(2,1)S(1)} %copy.63), channel_id=1, replica_groups=mesh['ctx'=8,'chan'=4] {'ctx'}, dimensions={2} | all-to-all | bytes 2097152 | tf_op jit(solution)/shard_map/all_to_all | solution.py:111
  173.4 0.5 copy.65
  174.6 0.5 copy.66
  175.3 0.4 fusion.32
  175.8 12.0 %all_to_all.47 = bf16[8,32,512]{2,1,0:T(8,128)(2,1)S(1)} all-to-all(bf16[8,32,512]{2,1,0:T(8,128)(2,1)S(1)} %copy.67), channel_id=1, replica_groups=mesh['ctx'=8,'chan'=4] {'ctx'}, dimensions={0} | all-to-all | bytes 524288 | tf_op jit(solution)/shard_map/all_to_all | solution.py:119
  187.8 4.8 %convolution_convert_fusion = bf16[256,4096]{1,0:T(8,128)(2,1)} fusion(bf16[512,4096]{1,0:T(8,128)(2,1)} %param.13, f32[3,256,512]{2,1,0:T(8,128)S(1)} %copy-done.1, bf16[256,512]{1,0:T(8,128)(2,1)S(1)} %bitcast.108), kind=kOutput, calls=%fused_computation.3 | convolution fusion | flops 1075183616 | bytes 7077888 | tf_op jit(solution)/shard_map/dot_general | solution.py:166
  192.6 29.7 %reduce-scatter.2.cloned.1.call-done = bf16[256,1024]{1,0:T(8,128)(2,1)} async-done(((bf16[256,4096]{1,0:T(8,128)(2,1)}), bf16[256,1024]{1,0:T(8,128)(2,1)}) %reduce-scatter.2.cloned.1.call-update) | async-done | bytes 524304 | tf_op jit(solution)/shard_map/reduce_scatter | solution.py:167
  (31 shorter events, 2.6 us)
Async XLA Ops:
  6.5 27.7 %all-gather.2.cloned.1.call-start = ((), (), s32[]{:S(2)}) async-start(), calls=%async_computation.5 | async-start | bytes 2621440 | tf_op jit(solution)/shard_map/all_gather | solution.py:126
  9.0 27.5 %copy-start.3 = (f32[4096]{0:T(1024)S(1)}, f32[4096]{0:T(1024)}, u32[]{:S(2)}) copy-start(f32[4096]{0:T(1024)} %param.8) | copy-start | bytes 49156
  34.2 2.3 copy-start.2
  43.1 4.7 %collective-permute-start = (bf16[3,2,512]{2,1,0:T(2,128)(2,1)S(1)}, bf16[3,2,512]{2,1,0:T(2,128)(2,1)S(1)}, u32[]{:S(2)}, u32[]{:S(2)}) collective-permute-start(bf16[3,2,512]{2,1,0:T(2,128)(2,1)S(1)} %slice.90), channel_id=1, source_target_pairs={{0,4},{4,8},{8,12},{12,16},{16,20},{20,24},{24,28},{1,5},{5,9},{9,... | collective-permute-start | bytes 18440 | tf_op jit(solution)/shard_map/ppermute | solution.py:23
  48.5 20.6 %copy-start = (f32[3,256,512]{2,1,0:T(8,128)}, f32[3,256,512]{2,1,0:T(8,128)S(1)}, u32[]{:S(2)}) copy-start(f32[3,256,512]{2,1,0:T(8,128)S(1)} %fusion.21) | copy-start | bytes 4718596
  74.1 51.4 %all-to-all-start.1 = ((bf16[2,2,16,32,512]{4,3,0,1,2:T(8,128)(2,1)}), bf16[2,2,16,32,512]{4,3,0,1,2:T(8,128)(2,1)S(1)}, u32[]{:S(2)}, u32[]{:S(2)}) async-start(bf16[2,2,16,32,512]{4,3,0,1,2:T(8,128)(2,1)} %copy.60), calls=%async_computation.1 | async-start | bytes 4194304 | tf_op jit(solution)/shard_map/all_to_all | solution.py:104
  77.8 144.6 %reduce-scatter.2.cloned.1.call-start = ((), (), s32[]{:S(2)}) async-start(), calls=%async_computation.6 | async-start | bytes 2621440 | tf_op jit(solution)/shard_map/reduce_scatter | solution.py:167
  174.6 13.3 %copy-start.1 = (f32[3,256,512]{2,1,0:T(8,128)S(1)}, f32[3,256,512]{2,1,0:T(8,128)}, u32[]{:S(2)}) copy-start(f32[3,256,512]{2,1,0:T(8,128)} %copy-done) | copy-start | bytes 4718596
Sparse Core Ops, SparseCore 0:
  8.9 25.2 all-gather.1
  192.8 29.5 reduce-scatter.1
where the time goes:
time: 230 us; the launch traced here: 229 us
  waiting for transfers between devices  101 us (44%)
  blocking collectives  61.2 us (27%)
  matrix products  29.5 us (13%)
  between operations  13.7 us (6%)
  other arithmetic  9.09 us (4%)
  local copies, waits for them, and re-layouts  7.54 us (3%)
  starting transfers between devices  7.23 us (3%)
    all_to_all x1, waiting for transfers between devices, halved_forward(): lax.all_to_all(shortened(spectra), 'ctx', split_axis=2, concat_axis=3, ti...  45.4 us
    reduce_scatter x1, waiting for transfers between devices, shards(): lax.psum_scatter(partial_sums.astype(jnp.bfloat16), 'chan', scatter_dimen...  29.7 us
    all_to_all x1, blocking collectives, halved_inverse(): lax.all_to_all(shortened(jnp.stack([spec_real, spec_imag], axis=0)), 'ctx...  29.3 us
    all_gather x1, waiting for transfers between devices, shards(): features_all = lax.all_gather(tokens, 'chan', axis=1, tiled=True)  23.8 us
    all_to_all x1, blocking collectives, halved_forward(): lax.all_to_all(signal[:, None].astype(jnp.bfloat16), 'ctx', split_axis=2,...  19.9 us
    all_to_all x1, blocking collectives, halved_inverse(): lax.all_to_all(shortened(real_rows), 'ctx', split_axis=0, concat_axis=1,...  12 us
    dot_general x1, matrix products, local_forward(): jnp.einsum('pj,fsjc->fspc', block_table, stacked, precision=highest)  7.95 us
    dot_general x1, matrix products, local_inverse(): jnp.einsum('jp,spc->sjc', block_table, stacked, precision=highest)  7.1 us
  transfers between devices with their start and end apart: 4, of which 4 were waited for; matrix products, arithmetic and copies ran while one was open for 2% of the time, Pallas kernels for 0%

commit v1 on v0

v1 whole, which is shorter than its diff:
```python
import math

import jax
import jax.numpy as jnp
from jax import lax
from jax.sharding import PartitionSpec as P

high = lax.Precision.HIGH


def from_behind(shard, axis, by):
    peers = lax.axis_size(axis)
    pairs = [(i, i + by) for i in range(peers) if 0 <= i + by < peers]
    return lax.ppermute(shard, axis, pairs)


def odd_tables(rows):
    steps = jnp.arange(rows, dtype=jnp.int32)
    turns = (2 * steps[:, None] + 1) * steps[None, :] % (4 * rows)
    angle = turns.astype(jnp.float32) * (math.pi / (2 * rows))
    return jnp.cos(angle), jnp.sin(angle)


def local_convolution(drive, kernel):
    rows = drive.shape[0]
    cos_table, sin_table = odd_tables(rows)
    forward = jnp.concatenate([cos_table, -sin_table], axis=0)
    both = jnp.concatenate([drive, kernel], axis=1)
    spectra = jnp.dot(forward, both, precision=high)
    width = drive.shape[1]
    dr, di = spectra[:rows, :width], spectra[rows:, :width]
    kr, ki = spectra[:rows, width:], spectra[rows:, width:]
    product = jnp.concatenate([dr * kr - di * ki, dr * ki + di * kr], axis=0)
    backward = jnp.concatenate([cos_table.T, -sin_table.T], axis=1) / rows
    return jnp.dot(backward, product, precision=high)


def shards(tokens, gain, in_weight, short_weight, residues, rates, out_weight):
    features_all = lax.all_gather(tokens, "chan", axis=1, tiled=True)
    wide_rows = features_all.astype(jnp.float32)
    scale_rms = lax.rsqrt(jnp.mean(wide_rows * wide_rows, axis=-1, keepdims=True) + 1e-06)
    normed = (wide_rows * scale_rms * gain).astype(jnp.bfloat16)
    projected = jnp.einsum(
        "td,gdc->gtc", normed, in_weight, preferred_element_type=jnp.float32
    ).astype(jnp.bfloat16)
    rows = projected.shape[1]
    rim_size = short_weight.shape[1] - 1
    rim_rows = from_behind(projected[:, rows - rim_size :, :], "ctx", 1)
    extended = jnp.concatenate([rim_rows, projected], axis=1).astype(jnp.float32)
    filtered = jnp.zeros((3, rows, projected.shape[2]), jnp.float32)
    for i in range(rim_size + 1):
        filtered = (
            filtered + short_weight[:, i][:, None, :] * extended[:, rim_size - i : rim_size - i + rows]
        )
    drive = filtered[1] * filtered[2]
    blocks = lax.axis_size("ctx")
    block = lax.axis_index("ctx")
    decay = rates / (rows * blocks)
    amplitude = residues * jnp.sqrt(-jnp.expm1(-2.0 * decay))
    steps = jnp.arange(rows, dtype=jnp.float32)[None, :, None]
    powers = jnp.exp(-decay[:, None, :] * steps)
    kernel = jnp.sum(amplitude[:, None, :] * powers, axis=0)
    state = jnp.sum(jnp.exp(-decay[:, None, :] * (rows - 1 - steps)) * drive[None], axis=1)
    states = lax.all_gather(state, "ctx", axis=0)
    behind = block - 1 - jnp.arange(blocks, dtype=jnp.int32)
    gaps = jnp.maximum(behind, 0).astype(jnp.float32)[:, None, None] * rows
    carried = jnp.where(behind[:, None, None] >= 0, jnp.exp(-decay[None] * gaps) * states, 0.0)
    carried = jnp.sum(carried, axis=0) * amplitude
    tail = jnp.sum(jnp.exp(-decay[:, None, :] * (steps + 1)) * carried[:, None, :], axis=0)
    convolved = local_convolution(drive, kernel) + tail
    gated_rows = (filtered[0] * convolved).astype(jnp.bfloat16)
    partial_sums = jnp.dot(gated_rows, out_weight, preferred_element_type=jnp.float32)
    return lax.psum_scatter(
        partial_sums.astype(jnp.bfloat16), "chan", scatter_dimension=1, tiled=True
    )


def solution(mesh):
    return jax.shard_map(
        shards,
        mesh=mesh,
        in_specs=(
            P("ctx", "chan"),
            P(),
            P(None, None, "chan"),
            P(None, None, "chan"),
            P(None, "chan"),
            P(None, "chan"),
            P("chan", None),
        ),
        out_specs=P("ctx", "chan"),
        check_vma=False,
    )
```

time: 230 us -> 131 us (0.57)
  waiting for transfers between devices: 101 us -> 55.7 us
  blocking collectives: 61.2 us -> 32.8 us
  matrix products: 29.5 us -> 13.1 us
  local copies, waits for them, and re-layouts: 7.54 us -> 1.09 us
  starting transfers between devices: 7.23 us -> 3.41 us
    all_to_all x3 -> x0, blocking collectives: 61.2 us -> none  [the longest x1 29.3 us: halved_inverse(): lax.all_to_all(shortened(jnp.stack([spec_real, spec_imag], axis=0)), 'ctx...]
    all_to_all x1 -> x0, waiting for transfers between devices: 45.4 us -> none  [halved_forward(): lax.all_to_all(shortened(spectra), 'ctx', split_axis=2, concat_axis=3, ti...]
    all_gather x0 -> x1, blocking collectives: none -> 32.8 us  [shards(): states = lax.all_gather(state, 'ctx', axis=0)]
    dot_general x6 -> x2, matrix products: 18.1 us -> 1.74 us  [the longest x1 1.04 us: local_convolution(): spectra = jnp.dot(forward, both, precision=high)]
    another operation x3 -> x0, local copies, waits for them, and re-layouts: 4.15 us -> none  [the longest x1 2.49 us: across_blocks(): return jnp.stack([real_part, imag_part], axis=1)]
    all_to_all x1 -> x0, starting transfers between devices: 3.64 us -> none  [halved_forward(): lax.all_to_all(shortened(spectra), 'ctx', split_axis=2, concat_axis=3, ti...]
    reduce_sum x1 -> x3, other arithmetic: 1.43 us -> 4.67 us  [the longest x1 3.07 us: shards(): kernel = jnp.sum(amplitude[:, None, :] * powers, axis=0)]
  transfers between devices with their start and end apart: 4 -> 3, of which waited for: 4 -> 3; matrix products, arithmetic and copies ran while one was open for 2% -> 3% of each run, Pallas kernels for 0% -> 0%
where the time goes in v1:
time: 131 us; the launch traced here: 130 us
  waiting for transfers between devices  55.7 us (43%)
  blocking collectives  32.8 us (25%)
  between operations  13.6 us (10%)
  matrix products  13.1 us (10%)
  other arithmetic  10.7 us (8%)
  starting transfers between devices  3.41 us (3%)
    all_gather x1, blocking collectives, shards(): states = lax.all_gather(state, 'ctx', axis=0)  32.8 us
    reduce_scatter x1, waiting for transfers between devices, shards(): lax.psum_scatter(partial_sums.astype(jnp.bfloat16), 'chan', scatter_dimen...  30.6 us
    all_gather x1, waiting for transfers between devices, shards(): features_all = lax.all_gather(tokens, 'chan', axis=1, tiled=True)  23.1 us
    dot_general x1, matrix products, shards(): jnp.einsum('td,gdc->gtc', normed, in_weight, preferred_element_type=jnp.f...  8.69 us
    ppermute x1, starting transfers between devices, from_behind(): return lax.ppermute(shard, axis, pairs)  3.37 us
    reduce_sum x1, other arithmetic, shards(): kernel = jnp.sum(amplitude[:, None, :] * powers, axis=0)  3.07 us
    dot_general x1, matrix products, shards(): jnp.dot(gated_rows, out_weight, preferred_element_type=jnp.float32)  2.67 us
  transfers between devices with their start and end apart: 3, of which 3 were waited for; matrix products, arithmetic and copies ran while one was open for 3% of the time, Pallas kernels for 0%

profile of v1, /device:TPU:0, one launch (start us, length us, event | category | flops | bytes accessed | tf_op | source)
XLA Modules:
  0.0 130.5 jit_solution(11205491284925012536)
XLA Ops:
  6.5 0.0 all-gather.3.cloned.1.call-start
  6.5 0.7 all-gather.3.cloned.1.call-update
  7.3 0.0 reduce-scatter.2.cloned.1.call-start
  7.4 0.9 fusion.51
  8.2 0.8 multiply_negate_fusion
  9.0 2.1 %fusion.45 = (f32[256,256]{1,0:T(8,128)S(1)}, f32[256,256]{1,0:T(8,128)S(1)}, f32[256,256]{1,0:T(8,128)S(1)}, f32[256,256]{1,0:T(8,128)S(1)}) fusion(s32[256]{0:T(256)S(1)} %multiply_add_fusion.1), kind=kLoop, calls=%fused_computation.65 | loop fusion | flops 1966080 | bytes 1049600 | tf_op jit(solution)/shard_map/cos | solution.py:21
  11.1 23.1 %all-gather.3.cloned.1.call-done = bf16[256,4096]{1,0:T(8,128)(2,1)} async-done(((bf16[256,1024]{1,0:T(8,128)(2,1)}), bf16[256,4096]{1,0:T(8,128)(2,1)}) %all-gather.3.cloned.1.call-update) | async-done | bytes 2097168 | tf_op jit(solution)/shard_map/all_gather | solution.py:39
  34.2 2.1 %fusion = f32[256]{0:T(256)S(1)} fusion(bf16[256,4096]{1,0:T(8,128)(2,1)} %all-gather.3.cloned.1.call-done), kind=kLoop, calls=%fused_computation.6 | loop fusion | flops 3145472 | bytes 2098176 | tf_op jit(solution)/shard_map/reduce_sum | solution.py:41
  36.3 8.7 %fusion.13 = bf16[3,256,512]{2,1,0:T(8,128)(2,1)S(1)} fusion(bf16[3,4096,512]{2,1,0:T(8,128)(2,1)} %param.9, bf16[256,4096]{1,0:T(8,128)(2,1)} %all-gather.3.cloned.1.call-done, f32[4096]{0:T(1024)} %param.8, f32[256]{0:T(256)S(1)} %add_rsqrt_fusion), kind=kOutput, calls=%fused_computation.19 | convolution fusion | flops 3225812992 | bytes 15483904 | tf_op jit(solution)/shard_map/td,gdc->gtc/dot_general | solution.py:43
  45.0 3.4 %collective-permute-start = (bf16[3,2,512]{2,1,0:T(2,128)(2,1)S(1)}, bf16[3,2,512]{2,1,0:T(2,128)(2,1)S(1)}, u32[]{:S(2)}, u32[]{:S(2)}) collective-permute-start(bf16[3,2,512]{2,1,0:T(2,128)(2,1)S(1)} %slice.56), channel_id=1, source_target_pairs={{0,4},{4,8},{8,12},{12,16},{16,20},{20,24},{24,28},{1,5},{5,9},{9,... | collective-permute-start | bytes 18440 | tf_op jit(solution)/shard_map/ppermute | solution.py:14
  48.4 1.3 %collective-permute-done = bf16[3,2,512]{2,1,0:T(2,128)(2,1)S(1)} collective-permute-done((bf16[3,2,512]{2,1,0:T(2,128)(2,1)S(1)}, bf16[3,2,512]{2,1,0:T(2,128)(2,1)S(1)}, u32[]{:S(2)}, u32[]{:S(2)}) %collective-permute-start) | collective-permute-done | bytes 6176 | tf_op jit(solution)/shard_map/ppermute | solution.py:14
  49.8 0.2 maximum_convert_fusion
  50.0 0.5 fusion.8
  50.5 0.0 copy-start
  50.5 0.0 copy-start.1
  50.5 0.1 fusion.25
  50.6 1.5 %multiply_reduce_fusion.1 = f32[16,512]{1,0:T(8,128)S(1)} fusion(f32[256,512]{1,0:T(8,128)S(1)} %fusion.25, f32[256]{0:T(256)S(1)} %iota_subtract_fusion, f32[16,512]{1,0:T(8,128)S(1)} %multiply_negate_fusion), kind=kLoop, calls=%fused_computation.1 | loop fusion | flops 6283264 | bytes 590848 | tf_op jit(solution)/shard_map/reduce_sum | solution.py:63
  52.1 32.8 %all-gather = f32[128,512]{1,0:T(8,128)S(1)} all-gather(f32[16,512]{1,0:T(8,128)S(1)} %multiply_reduce_fusion.1), channel_id=2, replica_groups=mesh['ctx'=8,'chan'=4] {'ctx'}, dimensions={0}, use_global_device_ids=true | all-gather | bytes 294912 | tf_op jit(solution)/shard_map/all_gather | solution.py:64
  84.9 0.1 select_reduce_fusion
  85.0 0.0 copy-done
  85.0 0.0 copy-done.1
  85.1 3.1 %multiply_reduce_fusion.2 = (f32[256,512]{1,0:T(8,128)S(1)}, f32[256,512]{1,0:T(8,128)S(1)}) fusion(f32[16,512]{1,0:T(8,128)S(1)} %multiply_negate_fusion, f32[16,512]{1,0:T(8,128)S(1)} %get-tuple-element.8, f32[16,512]{1,0:T(8,128)S(1)} %get-tuple-element.7, f32[256]{0:T(256)S(1)} %iota_add_fusion), kind=kLoop, calls=%fused_computation.2 | loop fusion | flops 12320768 | bytes 1147904 | tf_op jit(solution)/shard_map/reduce_sum | solution.py:62
  88.1 0.0 copy-start.2
  88.1 1.0 fusion.18
  89.2 0.2 multiply_subtract_fusion
  89.4 0.7 fusion.17
  90.1 0.2 copy-done.2
  90.3 2.7 %convolution_convert_fusion = bf16[256,4096]{1,0:T(8,128)(2,1)} fusion(bf16[256,512]{1,0:T(8,128)(2,1)S(1)} %fusion.17, bf16[512,4096]{1,0:T(8,128)(2,1)S(1)} %copy-done.2), kind=kOutput, calls=%fused_computation.5 | convolution fusion | flops 1074790400 | bytes 6553600 | tf_op jit(solution)/shard_map/dot_general | solution.py:72
  93.0 0.0 reduce-scatter.2.cloned.1.call-update
  93.0 30.6 %reduce-scatter.2.cloned.1.call-done = bf16[256,1024]{1,0:T(8,128)(2,1)} async-done(((bf16[256,4096]{1,0:T(8,128)(2,1)}), bf16[256,1024]{1,0:T(8,128)(2,1)}) %reduce-scatter.2.cloned.1.call-update) | async-done | bytes 524304 | tf_op jit(solution)/shard_map/reduce_scatter | solution.py:73
  (10 shorter events, 0.1 us)
Async XLA Ops:
  6.5 27.7 %all-gather.3.cloned.1.call-start = ((), (), s32[]{:S(2)}) async-start(), calls=%async_computation.1 | async-start | bytes 2621440 | tf_op jit(solution)/shard_map/all_gather | solution.py:39
  7.3 116.4 %reduce-scatter.2.cloned.1.call-start = ((), (), s32[]{:S(2)}) async-start(), calls=%async_computation.2 | async-start | bytes 2621440 | tf_op jit(solution)/shard_map/reduce_scatter | solution.py:73
  45.0 4.7 %collective-permute-start = (bf16[3,2,512]{2,1,0:T(2,128)(2,1)S(1)}, bf16[3,2,512]{2,1,0:T(2,128)(2,1)S(1)}, u32[]{:S(2)}, u32[]{:S(2)}) collective-permute-start(bf16[3,2,512]{2,1,0:T(2,128)(2,1)S(1)} %slice.56), channel_id=1, source_target_pairs={{0,4},{4,8},{8,12},{12,16},{16,20},{20,24},{24,28},{1,5},{5,9},{9,... | collective-permute-start | bytes 18440 | tf_op jit(solution)/shard_map/ppermute | solution.py:14
  50.5 34.5 %copy-start = (f32[16,512]{1,0:T(8,128)S(1)}, f32[16,512]{1,0:T(8,128)}, u32[]{:S(2)}) copy-start(f32[16,512]{1,0:T(8,128)} %param.12) | copy-start | bytes 98308
  50.5 34.5 %copy-start.1 = (f32[16,512]{1,0:T(8,128)S(1)}, f32[16,512]{1,0:T(8,128)}, u32[]{:S(2)}) copy-start(f32[16,512]{1,0:T(8,128)} %param.11) | copy-start | bytes 98308
  88.1 2.2 %copy-start.2 = (bf16[512,4096]{1,0:T(8,128)(2,1)S(1)}, bf16[512,4096]{1,0:T(8,128)(2,1)}, u32[]{:S(2)}) copy-start(bf16[512,4096]{1,0:T(8,128)(2,1)} %param.13) | copy-start | bytes 12582916
Sparse Core Ops, SparseCore 0:
  8.9 25.2 all-gather.2
  93.1 30.4 reduce-scatter.1

commit v2 on v1

v2 whole, which is shorter than its diff:
```python
import functools
import math

import jax
import jax.numpy as jnp
import numpy as np
from jax import lax
from jax.experimental import pallas as pl
from jax.experimental.pallas import tpu as pltpu
from jax.sharding import PartitionSpec as P

RIM = 16
MESH = pl.DeviceIdType.MESH
f32 = jnp.float32
bf16 = jnp.bfloat16


def tables(rows):
    steps = np.arange(rows)
    turns = ((2 * steps[:, None] + 1) * steps[None, :]) % (4 * rows)
    angle = turns * (math.pi / (2 * rows))
    cos, sin = np.cos(angle), np.sin(angle)
    forward = np.concatenate([cos, -sin], axis=0)
    flipped = np.eye(rows)[::-1]
    both = np.concatenate([forward, flipped], axis=0)
    backward = np.concatenate([cos.T, -sin.T], axis=1) / rows
    return forward.astype(np.float32), both.astype(np.float32), backward.astype(np.float32)


def one_less_exp(x):
    series = jnp.full_like(x, 1.0 / 5040.0)
    for term in (720.0, 120.0, 24.0, 6.0, 2.0, 1.0):
        series = 1.0 / term - x * series
    return jnp.where(x < 0.25, x * series, 1.0 - jnp.exp(-x))


def layer(
    n_ctx,
    tok,
    gain,
    w_hbm,
    short,
    residues,
    rates,
    ow_hbm,
    fwd_hbm,
    both_hbm,
    back_hbm,
    out,
    buf,
    w,
    ow,
    fwd,
    both,
    back,
    acc,
    squares,
    ext,
    gate,
    powers,
    spec_k,
    spec,
    drive,
    conv,
    amp,
    state_out,
    state_in,
    carry,
    gated,
    gated_in,
    sent,
    landed,
    local_sem,
    g_send,
    g_recv,
    h_send,
    h_recv,
    o_send,
    o_recv,
    s_send,
    s_recv,
    r_send,
    r_recv,
):
    rows, width = tok.shape
    chans = w_hbm.shape[2]
    modes = rates.shape[0]
    cut = width // 4
    length = rows * n_ctx
    me = lax.axis_index("chan")
    ctx = lax.axis_index("ctx")
    sib = me + 1 - 2 * lax.rem(me, 2)
    acr = lax.rem(me + 2, 4)
    dia = lax.rem(sib + 2, 4)
    owners = (me, sib, acr, dia)

    def local(src, dst, k):
        copy = pltpu.make_async_copy(src, dst, local_sem.at[k])
        copy.start()
        return copy

    def remote(src, dst, send, recv, peer):
        return pltpu.make_async_remote_copy(
            src_ref=src, dst_ref=dst, send_sem=send, recv_sem=recv, device_id=peer, device_id_type=MESH
        )

    def cols(block, size):
        return pl.ds(pl.multiple_of(block * size, size), size)

    own_tokens = local(tok, buf.at[0, 0:rows], 0)
    fwd_copy = local(fwd_hbm, fwd, 1)
    w_copies = [
        local(w_hbm.at[:, cols(owners[s], width), :], w.at[:, s * width : (s + 1) * width, :], 2 + s)
        for s in range(4)
    ]
    both_copy = local(both_hbm, both, 6)
    back_copy = local(back_hbm, back, 7)
    ow_copies = [local(ow_hbm.at[:, cols(b, width)], ow.at[0, i], 8 + i) for i, b in enumerate((me, acr))]

    barrier = pltpu.get_barrier_semaphore()
    pl.semaphore_signal(barrier, inc=1, device_id={"chan": sib}, device_id_type=MESH)
    pl.semaphore_signal(barrier, inc=1, device_id={"chan": acr}, device_id_type=MESH)
    for rel in range(1, n_ctx):
        peer = lax.rem(ctx + rel, n_ctx)
        pl.semaphore_signal(barrier, inc=1, device_id={"ctx": peer}, device_id_type=MESH)
    pl.semaphore_wait(barrier, n_ctx + 1)

    across = []
    for c in range(4):
        here = slice(c * cut, (c + 1) * cut)
        across.append(
            remote(tok.at[:, here], buf.at[2, 0:rows, here], g_send.at[c], g_recv.at[c], {"chan": acr})
        )
    beside = remote(tok, buf.at[1, 0:rows], g_send.at[4], g_recv.at[4], {"chan": sib})
    rim_on = remote(
        tok.at[rows - RIM : rows, :],
        buf.at[0, rows : rows + RIM],
        h_send.at[0],
        h_recv.at[0],
        {"ctx": lax.rem(ctx + 1, n_ctx)},
    )
    rim_on.start()
    across[0].start()
    beside.start()
    rim_here = buf.at[0, rows : rows + RIM]
    rim_on.wait_recv()
    rim_across = remote(rim_here, buf.at[2, rows : rows + RIM], h_send.at[1], h_recv.at[1], {"chan": acr})
    rim_beside = remote(rim_here, buf.at[1, rows : rows + RIM], h_send.at[2], h_recv.at[2], {"chan": sib})
    rim_across.start()
    rim_beside.start()
    for c in range(1, 4):
        across[c].start()
    ow_out = []
    for i, b in enumerate((sib, dia)):
        copy = remote(ow_hbm.at[:, cols(b, width)], ow.at[1, i], o_send.at[i], o_recv.at[i], {"chan": sib})
        copy.start()
        ow_out.append(copy)

    decay_all = rates[...] * (1.0 / length)
    amp[...] = residues[...] * jnp.sqrt(one_less_exp(2.0 * decay_all))
    conv[...] = jnp.zeros_like(conv)
    eighth = lax.broadcasted_iota(jnp.int32, (8, chans), 0).astype(f32)
    groups = lax.broadcasted_iota(jnp.int32, (rows // 8, chans), 0).astype(f32) * 8.0

    def build(m, _):
        decay = rates[pl.ds(m, 1), :] * (1.0 / length)
        fine = jnp.exp(-decay * eighth)
        coarse = jnp.exp(-decay * groups)
        strength = amp[pl.ds(m, 1), :]
        for a in range(rows // 8):
            here = slice(a * 8, a * 8 + 8)
            value = fine * coarse[a : a + 1, :]
            powers[m, here, :] = value
            conv[here, :] += strength * value
        return 0

    lax.fori_loop(0, modes, build, 0)

    squares[...] = jnp.zeros_like(squares)

    def accumulate(slot, start, size, first):
        x = buf[slot, :, start : start + size].astype(f32)
        part = squares[...]
        for k in range(0, size, 128):
            piece = x[:, k : k + 128]
            part = part + piece * piece
        squares[...] = part
        scaled = (x * gain[pl.ds(owners[slot], 1), start : start + size]).astype(bf16)
        for g in range(3):
            base = slot * width + start
            term = jnp.dot(scaled, w[g, base : base + size, :], preferred_element_type=f32)
            if first:
                acc[g] = term
            else:
                acc[g] += term

    own_tokens.wait()
    w_copies[0].wait()
    accumulate(0, 0, width, True)
    across[0].wait_recv()
    onward = [
        remote(
            buf.at[2, 0:rows, c * cut : (c + 1) * cut],
            buf.at[3, 0:rows, c * cut : (c + 1) * cut],
            g_send.at[5 + c],
            g_recv.at[5 + c],
            {"chan": sib},
        )
        for c in range(4)
    ]
    onward[0].start()
    rim_across.wait_recv()
    rim_onward = remote(
        buf.at[2, rows : rows + RIM], buf.at[3, rows : rows + RIM], h_send.at[3], h_recv.at[3], {"chan": sib}
    )
    rim_onward.start()
    rim_beside.wait_recv()
    beside.wait_recv()
    w_copies[1].wait()
    accumulate(1, 0, width, False)

    fwd_copy.wait()
    spec_k[...] = jnp.dot(
        fwd[...], conv[...], preferred_element_type=f32, precision=lax.Precision.HIGHEST
    )

    w_copies[2].wait()
    w_copies[3].wait()
    for c in range(4):
        if c:
            across[c].wait_recv()
            onward[c].start()
        accumulate(2, c * cut, cut, False)
        if c == 0:
            rim_onward.wait_recv()
        onward[c].wait_recv()
        accumulate(3, c * cut, cut, False)

    mean = jnp.sum(squares[...], axis=1, keepdims=True) * (1.0 / (4 * width))
    scale = lax.rsqrt(mean + 1e-06)
    keep = jnp.where(ctx > 0, 1.0, 0.0)
    for g in range(3):
        ext[g, 0:8, :] = (acc[g, rows + 8 : rows + 16, :] * scale[rows + 8 : rows + 16]).astype(bf16).astype(
            f32
        ) * keep
        ext[g, 8 : rows + 8, :] = (acc[g, 0:rows, :] * scale[0:rows]).astype(bf16).astype(f32)
    step = 64
    for r in range(0, rows, step):
        mixed = []
        for g in range(3):
            total = short[g, 0:1, :] * ext[g, r + 8 : r + 8 + step, :]
            total = total + short[g, 1:2, :] * ext[g, r + 7 : r + 7 + step, :]
            total = total + short[g, 2:3, :] * ext[g, r + 6 : r + 6 + step, :]
            mixed.append(total)
        gate[r : r + step, :] = mixed[0]
        drive[r : r + step, :] = (mixed[1] * mixed[2]).astype(bf16)

    both_copy.wait()
    spec[...] = jnp.dot(both[...], drive[...], preferred_element_type=f32)

    for q in range(modes // 4):
        for lane in range(0, chans, 128):
            sums = [jnp.zeros((8, 128), f32) for _ in range(4)]
            for r in range(0, rows, 8):
                back_drive = spec[2 * rows + r : 2 * rows + r + 8, lane : lane + 128]
                for k in range(4):
                    sums[k] = sums[k] + powers[q * 4 + k, r : r + 8, lane : lane + 128] * back_drive
            for k in range(4):
                carry[q * 4 + k : q * 4 + k + 1, lane : lane + 128] = jnp.sum(sums[k], axis=0, keepdims=True)

    state_out[...] = carry[...].astype(bf16)
    states = []
    for rel in range(1, n_ctx):
        copy = remote(
            state_out,
            state_in.at[rel - 1],
            s_send.at[rel - 1],
            s_recv.at[rel - 1],
            {"ctx": lax.rem(ctx + rel, n_ctx)},
        )
        copy.start()
        states.append(copy)

    for r in range(0, rows, step):
        re, im = slice(r, r + step), slice(rows + r, rows + r + step)
        dr, di, kr, ki = spec[re, :], spec[im, :], spec_k[re, :], spec_k[im, :]
        spec[re, :] = dr * kr - di * ki
        spec[im, :] = dr * ki + di * kr
    back_copy.wait()
    conv[...] = jnp.dot(
        back[...], spec[0 : 2 * rows, :].astype(bf16), preferred_element_type=f32
    )

    block_decay = jnp.exp(-decay_all * rows)
    total = jnp.zeros((modes, chans), f32)
    for rel in range(n_ctx - 1, 0, -1):
        states[rel - 1].wait_recv()
        came = state_in[rel - 1].astype(f32)
        total = total * block_decay + came * jnp.where(ctx >= rel, 1.0, 0.0)
    carry[...] = total * amp[...] * jnp.exp(-decay_all)

    half = rows // 2
    shares = []
    for h in range(2):

        def tail(i, _, h=h):
            r = pl.multiple_of(h * half + i * 16, 16)
            here = pl.ds(r, 16)
            for lane in range(0, chans, 128):
                ln = slice(lane, lane + 128)
                total = conv[here, ln]
                for m in range(modes):
                    total = total + carry[m : m + 1, ln] * powers[m, here, ln]
                gated[here, ln] = (gate[here, ln] * total).astype(bf16)
            return 0

        lax.fori_loop(0, half // 16, tail, 0)
        share = remote(
            gated.at[h * half : (h + 1) * half],
            gated_in.at[h * half : (h + 1) * half],
            r_send.at[h],
            r_recv.at[h],
            {"chan": sib},
        )
        share.start()
        shares.append(share)

    for copy in ow_copies:
        copy.wait()
    for copy in ow_out:
        copy.wait_recv()
    wide = width // 2
    results = []
    for h in range(2):
        shares[h].wait_recv()
        hr = slice(h * half, (h + 1) * half)
        for j in range(2):
            jc = slice(j * wide, (j + 1) * wide)
            k = h * 2 + j
            part = jnp.dot(gated[hr, :], ow[0, 1, :, jc], preferred_element_type=f32)
            part = part + jnp.dot(gated_in[hr, :], ow[1, 1, :, jc], preferred_element_type=f32)
            sent[hr, jc] = part.astype(bf16)
            copy = remote(
                sent.at[hr, jc], landed.at[hr, jc], r_send.at[2 + k], r_recv.at[2 + k], {"chan": acr}
            )
            copy.start()
            results.append(copy)
    for j in range(2):
        jc = slice(j * wide, (j + 1) * wide)
        kept = jnp.dot(gated[...], ow[0, 0, :, jc], preferred_element_type=f32)
        kept = kept + jnp.dot(gated_in[...], ow[1, 0, :, jc], preferred_element_type=f32)
        acc[j, 0:rows, :] = kept
    for h in range(2):
        hr = slice(h * half, (h + 1) * half)
        for j in range(2):
            jc = slice(j * wide, (j + 1) * wide)
            results[h * 2 + j].wait_recv()
            out[hr, jc] = (acc[j, hr, :] + landed[hr, jc].astype(f32)).astype(bf16)

    for copy in across + onward + states + shares + results + ow_out:
        copy.wait_send()
    for copy in (beside, rim_on, rim_across, rim_beside, rim_onward):
        copy.wait_send()


def shards(n_ctx, tokens, gain, in_weight, short_weight, residues, rates, out_weight):
    rows, width = tokens.shape
    chans = in_weight.shape[2]
    modes = rates.shape[0]
    forward, both, backward = tables(rows)
    tall = rows + RIM
    vmem = pl.BlockSpec(memory_space=pltpu.VMEM)
    hbm = pl.BlockSpec(memory_space=pl.ANY)
    dma = pltpu.SemaphoreType.DMA
    return pl.pallas_call(
        functools.partial(layer, n_ctx),
        out_shape=jax.ShapeDtypeStruct((rows, width), bf16),
        in_specs=[hbm, vmem, hbm, vmem, vmem, vmem, hbm, hbm, hbm, hbm],
        out_specs=vmem,
        scratch_shapes=[
            pltpu.VMEM((4, tall, width), bf16),
            pltpu.VMEM((3, 4 * width, chans), bf16),
            pltpu.VMEM((2, 2, chans, width), bf16),
            pltpu.VMEM((2 * rows, rows), f32),
            pltpu.VMEM((3 * rows, rows), bf16),
            pltpu.VMEM((rows, 2 * rows), bf16),
            pltpu.VMEM((3, tall, chans), f32),
            pltpu.VMEM((tall, 128), f32),
            pltpu.VMEM((3, rows + 8, chans), f32),
            pltpu.VMEM((rows, chans), f32),
            pltpu.VMEM((modes, rows, chans), f32),
            pltpu.VMEM((2 * rows, chans), f32),
            pltpu.VMEM((3 * rows, chans), f32),
            pltpu.VMEM((rows, chans), bf16),
            pltpu.VMEM((rows, chans), f32),
            pltpu.VMEM((modes, chans), f32),
            pltpu.VMEM((modes, chans), bf16),
            pltpu.VMEM((n_ctx - 1, modes, chans), bf16),
            pltpu.VMEM((modes, chans), f32),
            pltpu.VMEM((rows, chans), bf16),
            pltpu.VMEM((rows, chans), bf16),
            pltpu.VMEM((rows, width), bf16),
            pltpu.VMEM((rows, width), bf16),
            dma((10,)),
            dma((9,)),
            dma((9,)),
            dma((4,)),
            dma((4,)),
            dma((2,)),
            dma((2,)),
            dma((n_ctx - 1,)),
            dma((n_ctx - 1,)),
            dma((6,)),
            dma((6,)),
        ],
        compiler_params=pltpu.CompilerParams(
            collective_id=0, has_side_effects=True, vmem_limit_bytes=60 * 1024 * 1024
        ),
        name="hyena_layer",
    )(
        tokens,
        gain.reshape(4, width),
        in_weight,
        short_weight,
        residues,
        rates,
        out_weight,
        jnp.asarray(forward),
        jnp.asarray(both, dtype=bf16),
        jnp.asarray(backward, dtype=bf16),
    )


def solution(mesh):
    return jax.shard_map(
        functools.partial(shards, mesh.shape["ctx"]),
        mesh=mesh,
        in_specs=(
            P("ctx", "chan"),
            P(),
            P(None, None, "chan"),
            P(None, None, "chan"),
            P(None, "chan"),
            P(None, "chan"),
            P("chan", None),
        ),
        out_specs=P("ctx", "chan"),
        check_vma=False,
    )
```

time: 131 us -> 47.2 us (0.36)
  waiting for transfers between devices: 55.7 us -> 0 us
  Pallas kernels: 0 us -> 43.8 us
  blocking collectives: 32.8 us -> 0 us
  between operations: 13.6 us -> 0.01 us
  matrix products: 13.1 us -> 0 us
  other arithmetic: 10.7 us -> 0 us
  starting transfers between devices: 3.41 us -> 0 us
  local copies, waits for them, and re-layouts: 1.09 us -> 3.2 us
    pallas_call x0 -> x1, Pallas kernels: none -> 43.8 us  [shards(): pl.pallas_call(functools.partial(layer, n_ctx), out_shape=jax.ShapeDtypeS...]
    all_gather x1 -> x0, blocking collectives: 32.8 us -> none  [shards(): states = lax.all_gather(state, 'ctx', axis=0)]
    reduce_scatter x1 -> x0, waiting for transfers between devices: 30.6 us -> none  [shards(): lax.psum_scatter(partial_sums.astype(jnp.bfloat16), 'chan', scatter_dimen...]
    all_gather x1 -> x0, waiting for transfers between devices: 23.1 us -> none  [shards(): features_all = lax.all_gather(tokens, 'chan', axis=1, tiled=True)]
    dot_general x4 -> x0, matrix products: 13.1 us -> none  [the longest x1 8.69 us: shards(): jnp.einsum('td,gdc->gtc', normed, in_weight, preferred_element_type=jnp.f...]
    reduce_sum x4 -> x0, other arithmetic: 6.75 us -> none  [the longest x1 3.07 us: shards(): kernel = jnp.sum(amplitude[:, None, :] * powers, axis=0)]
    ppermute x1 -> x0, starting transfers between devices: 3.37 us -> none  [from_behind(): return lax.ppermute(shard, axis, pairs)]
    cos x1 -> x0, other arithmetic: 2.12 us -> none  [odd_tables(): return (jnp.cos(angle), jnp.sin(angle))]
  transfers between devices with their start and end apart: 3 -> 0, of which waited for: 3 -> 0; matrix products, arithmetic and copies ran while one was open for 3% -> 0% of each run, Pallas kernels for 0% -> 0%
where the time goes in v2:
time: 47.2 us; the launch traced here: 47 us
  Pallas kernels  43.8 us (93%)
  local copies, waits for them, and re-layouts  3.2 us (7%)
    pallas_call x1, Pallas kernels, shards(): pl.pallas_call(functools.partial(layer, n_ctx), out_shape=jax.ShapeDtypeS...  43.8 us
    unnamed x1, local copies, waits for them, and re-layouts  1.87 us
    reshape x1, local copies, waits for them, and re-layouts, shards(): gain.reshape(4, width)  1.33 us

profile of v2, /device:TPU:0, one launch (start us, length us, event | category | flops | bytes accessed | tf_op | source)
XLA Modules:
  0.0 47.0 jit_solution(9210016602847259633)
XLA Ops:
  0.0 1.3 %reshape.3.gain = f32[4,1024]{1,0:T(4,128)} reshape(f32[4096]{0:T(1024)} %param.11) | data formatting | bytes 32768 | tf_op jit(solution)/shard_map/reshape | solution.py:422
  1.3 43.8 %hyena_layer.1 = bf16[256,1024]{1,0:T(8,128)(2,1)} custom-call(bf16[256,1024]{1,0:T(8,128)(2,1)} %tok.1, f32[4,1024]{1,0:T(4,128)} %reshape.3.gain, bf16[3,4096,512]{2,1,0:T(8,128)(2,1)} %w_hbm.1, f32[3,3,512]{2,1,0:T(4,128)} %short.1, f32[16,512]{1,0:T(8,128)} %residues.1, f32[16,512]{1,0:T(8,128)} %rates.1, bf16[512,4096]{1,0:T(8,128)(2,1)} %ow_hbm.1, ...), custom_call_target="tpu_custom_call" | custom-call | tf_op jit(solution)/shard_map/hyena_layer/pallas_call | solution.py:375
  45.1 1.9 %copy.12 = bf16[256,1024]{1,0:T(8,128)(2,1)} copy(bf16[256,1024]{1,0:T(8,128)(2,1)} %hyena_layer.1) | data formatting | bytes 1048576

commit v3 on v2

--- a/solution.py
+++ b/solution.py
@@ -81,6 +81,7 @@
     s_recv,
     r_send,
     r_recv,
+    near_sem,
 ):
     rows, width = tok.shape
     chans = w_hbm.shape[2]
@@ -107,6 +108,20 @@
     def cols(block, size):
         return pl.ds(pl.multiple_of(block * size, size), size)
 
+    def greet(sem, far):
+        @pl.when(ctx + far < n_ctx)
+        def _():
+            pl.semaphore_signal(sem, inc=1, device_id={"ctx": ctx + far}, device_id_type=MESH)
+
+        @pl.when(ctx >= far)
+        def _():
+            pl.semaphore_signal(sem, inc=1, device_id={"ctx": ctx - far}, device_id_type=MESH)
+
+    def meet(sem, far, others=0):
+        ahead = 1 - lax.div(ctx + far, n_ctx)
+        behind = lax.div(ctx + n_ctx - far, n_ctx)
+        pl.semaphore_wait(sem, others + ahead + behind)
+
     own_tokens = local(tok, buf.at[0, 0:rows], 0)
     fwd_copy = local(fwd_hbm, fwd, 1)
     w_copies = [
@@ -120,10 +135,20 @@
     barrier = pltpu.get_barrier_semaphore()
     pl.semaphore_signal(barrier, inc=1, device_id={"chan": sib}, device_id_type=MESH)
     pl.semaphore_signal(barrier, inc=1, device_id={"chan": acr}, device_id_type=MESH)
-    for rel in range(1, n_ctx):
-        peer = lax.rem(ctx + rel, n_ctx)
-        pl.semaphore_signal(barrier, inc=1, device_id={"ctx": peer}, device_id_type=MESH)
-    pl.semaphore_wait(barrier, n_ctx + 1)
+    greet(barrier, 1)
+    meet(barrier, 1, 2)
+
+    reach = []
+    while sum(reach) + 1 < n_ctx - 1:
+        reach.append(2 ** len(reach))
+
+    def widen(k):
+        if 0 <= k - 1 < len(reach):
+            meet(near_sem.at[k - 1], reach[k - 1])
+        if k < len(reach):
+            greet(near_sem.at[k], reach[k])
+
+    widen(0)
 
     across = []
     for c in range(4):
@@ -139,11 +164,23 @@
         h_recv.at[0],
         {"ctx": lax.rem(ctx + 1, n_ctx)},
     )
-    rim_on.start()
+
+    @pl.when(ctx + 1 < n_ctx)
+    def _():
+        rim_on.start()
+
     across[0].start()
     beside.start()
     rim_here = buf.at[0, rows : rows + RIM]
-    rim_on.wait_recv()
+
+    @pl.when(ctx > 0)
+    def _():
+        rim_on.wait_recv()
+
+    @pl.when(ctx == 0)
+    def _():
+        buf[0, rows : rows + RIM] = jnp.zeros((RIM, width), bf16)
+
     rim_across = remote(rim_here, buf.at[2, rows : rows + RIM], h_send.at[1], h_recv.at[1], {"chan": acr})
     rim_beside = remote(rim_here, buf.at[1, rows : rows + RIM], h_send.at[2], h_recv.at[2], {"chan": sib})
     rim_across.start()
@@ -175,6 +212,7 @@
         return 0
 
     lax.fori_loop(0, modes, build, 0)
+    widen(1)
 
     squares[...] = jnp.zeros_like(squares)
 
@@ -185,7 +223,7 @@
             piece = x[:, k : k + 128]
             part = part + piece * piece
         squares[...] = part
-        scaled = (x * gain[pl.ds(owners[slot], 1), start : start + size]).astype(bf16)
+        scaled = (x * gain[cols(owners[slot] * (width // size) + start // size, size)][None, :]).astype(bf16)
         for g in range(3):
             base = slot * width + start
             term = jnp.dot(scaled, w[g, base : base + size, :], preferred_element_type=f32)
@@ -197,6 +235,7 @@
     own_tokens.wait()
     w_copies[0].wait()
     accumulate(0, 0, width, True)
+    widen(2)
     across[0].wait_recv()
     onward = [
         remote(
@@ -218,6 +257,7 @@
     beside.wait_recv()
     w_copies[1].wait()
     accumulate(1, 0, width, False)
+    widen(3)
 
     fwd_copy.wait()
     spec_k[...] = jnp.dot(
@@ -235,6 +275,7 @@
             rim_onward.wait_recv()
         onward[c].wait_recv()
         accumulate(3, c * cut, cut, False)
+        widen(4 + c)
 
     mean = jnp.sum(squares[...], axis=1, keepdims=True) * (1.0 / (4 * width))
     scale = lax.rsqrt(mean + 1e-06)
@@ -278,8 +319,12 @@
             s_recv.at[rel - 1],
             {"ctx": lax.rem(ctx + rel, n_ctx)},
         )
-        copy.start()
         states.append(copy)
+
+        @pl.when(ctx + rel < n_ctx)
+        def _(copy=copy):
+            copy.start()
+
 
     for r in range(0, rows, step):
         re, im = slice(r, r + step), slice(rows + r, rows + r + step)
@@ -292,12 +337,15 @@
     )
 
     block_decay = jnp.exp(-decay_all * rows)
-    total = jnp.zeros((modes, chans), f32)
+    carry[...] = jnp.zeros_like(carry)
     for rel in range(n_ctx - 1, 0, -1):
-        states[rel - 1].wait_recv()
-        came = state_in[rel - 1].astype(f32)
-        total = total * block_decay + came * jnp.where(ctx >= rel, 1.0, 0.0)
-    carry[...] = total * amp[...] * jnp.exp(-decay_all)
+        @pl.when(ctx >= rel)
+        def _(rel=rel):
+            states[rel - 1].wait_recv()
+            came = state_in[rel - 1].astype(f32)
+            carry[...] = carry[...] * block_decay + came
+
+    carry[...] = carry[...] * amp[...] * jnp.exp(-decay_all)
 
     half = rows // 2
     shares = []
@@ -357,10 +405,17 @@
             results[h * 2 + j].wait_recv()
             out[hr, jc] = (acc[j, hr, :] + landed[hr, jc].astype(f32)).astype(bf16)
 
-    for copy in across + onward + states + shares + results + ow_out:
+    for copy in across + onward + shares + results + ow_out:
         copy.wait_send()
-    for copy in (beside, rim_on, rim_across, rim_beside, rim_onward):
+    for copy in (beside, rim_across, rim_beside, rim_onward):
         copy.wait_send()
+    for rel in range(1, n_ctx):
+
+        @pl.when(ctx + rel < n_ctx)
+        def _(rel=rel):
+            states[rel - 1].wait_send()
+            if rel == 1:
+                rim_on.wait_send()
 
 
 def shards(n_ctx, tokens, gain, in_weight, short_weight, residues, rates, out_weight):
@@ -412,6 +467,7 @@
             dma((n_ctx - 1,)),
             dma((6,)),
             dma((6,)),
+            pltpu.SemaphoreType.REGULAR((8,)),
         ],
         compiler_params=pltpu.CompilerParams(
             collective_id=0, has_side_effects=True, vmem_limit_bytes=60 * 1024 * 1024
@@ -419,7 +475,7 @@
         name="hyena_layer",
     )(
         tokens,
-        gain.reshape(4, width),
+        gain,
         in_weight,
         short_weight,
         residues,

time: 47.2 us -> 43.4 us (0.919)
  the two profiles are of different devices: /device:TPU:0 before, /device:TPU:25 now
where the time goes in v3:
time: 43.4 us; the launch traced here: 43.2 us
  Pallas kernels  41.3 us (95%)
  local copies, waits for them, and re-layouts  1.87 us (4%)
    pallas_call x1, Pallas kernels, shards(): pl.pallas_call(functools.partial(layer, n_ctx), out_shape=jax.ShapeDtypeS...  41.3 us
    unnamed x1, local copies, waits for them, and re-layouts  1.87 us

profile of v3, /device:TPU:25, one launch (start us, length us, event | category | flops | bytes accessed | tf_op | source)
XLA Modules:
  0.0 43.2 jit_solution(12700700326305940460)
XLA Ops:
  0.0 41.3 %hyena_layer.1 = bf16[256,1024]{1,0:T(8,128)(2,1)} custom-call(bf16[256,1024]{1,0:T(8,128)(2,1)} %tok.1, f32[4096]{0:T(1024)} %gain.1, bf16[3,4096,512]{2,1,0:T(8,128)(2,1)} %w_hbm.1, f32[3,3,512]{2,1,0:T(4,128)} %short.1, f32[16,512]{1,0:T(8,128)} %residues.1, f32[16,512]{1,0:T(8,128)} %rates.1, bf16[512,4096]{1,0:T(8,128)(2,1)} %ow_hbm.1, ...), custom_call_target="tpu_custom_call" | custom-call | tf_op jit(solution)/shard_map/hyena_layer/pallas_call | solution.py:430
  41.3 1.9 %copy.12 = bf16[256,1024]{1,0:T(8,128)(2,1)} copy(bf16[256,1024]{1,0:T(8,128)(2,1)} %hyena_layer.1) | data formatting | bytes 1048576
